TPU v7x, 32 devices: a whole 2x2x4 slice. The times are simulated.
32 devices in a mesh: groups: 2 (over y), blk: 4 (over z), subj: 4 (over x, core).
Axes of the slice: x: 2, y: 2, z: 4, core: 2. Of those that a mesh axis runs over, the one named last changes fastest.
Arguments:
- template_verts: float32 [3, 2048], P(None, ('groups', 'blk')), parts along dimension 1, may hold values from -6 to 6
- template_tris: int32 [3, 2048], P(None, ('groups', 'blk')), parts along dimension 1, may hold values from 0 to 255
- local_pairs: int32 [8, 2], P('blk'), may hold values 0 or 1
- partner_blocks: int32 [4, 8], P(None, 'blk'), may hold values from 0 to 1, as said below
- controls: float32 [3, 8192], replicated, may hold values from -6 to 6
- momenta: float32 [128, 3, 8192], P(('groups', 'subj')), parts along dimension 0, may hold values from -0.06 to 0.06
- target_verts: float32 [128, 3, 1024], P(('groups', 'subj'), None, 'blk'), parts along dimension 0, may hold values from -6 to 6
- target_tris: int32 [128, 3, 1024], P(('groups', 'subj'), None, 'blk'), parts along dimension 0, may hold values from 0 to 255
Outputs:
- template_grad: float32 [3, 2048], P(None, ('groups', 'blk')), parts along dimension 1
- momenta_grad: float32 [128, 3, 8192], P(('groups', 'subj'), None, 'blk'), parts along dimension 0
There are 2 independent parts, one for each index of `groups`. A program takes and returns all parts, laid end to end along the dimension named above; an argument that names none is the same for every part. Nothing has to cross between parts.
Inputs may be any that keep to these rules, and one draw needn't show every extreme that they name: Corner k of template triangle t is template vertex (t // 256) * 256 + template_tris[k, t]; corners of one triangle may coincide. Corner k of triangle t of subject s is its vertex (t // 256) * 256 + target_tris[s, k, t]; corners may coincide. `partner_blocks`: for each r, shard d and its mate shard d XOR 2^(r mod L), the entries of the 2 blocks of d form a permutation of 0 to 1, and those of the mate shard its inverse, so that the pairing of blocks is mutual.
All inputs are finite; a program needn't handle non-finite values. No bound on the sum of `local_pairs` on one device may be relied on, other than what follows from the above.
Results may differ from a plain program's by a relative error of at most 0.0001.
Values sent between devices are 32-bit elements; how exact they have to be, the bound alone decides.
A program may use at most 64 MiB of HBM per device.

v0:
```python
import functools
import math

import jax
import jax.numpy as jnp
from jax import lax
from jax.experimental import pallas as pl
from jax.experimental.pallas import tpu as pltpu
from jax.sharding import PartitionSpec as P

AREA_SQ = 0.25
SCALE = math.sqrt(math.log2(math.e))
LANES = 128
MESH = pl.DeviceIdType.MESH
f32, bf16 = jnp.float32, jnp.bfloat16
NT = (((1,), (1,)), ((), ()))
NN = (((1,), (0,)), ((), ()))


def split(value):
    high = value.astype(bf16)
    return high, (value - high.astype(f32)).astype(bf16)


def mxu(a, b, dims):
    return lax.dot_general(a, b, dims, preferred_element_type=f32)


def pick_lanes(halves, indices):
    out = []
    for idx in indices:
        low = idx & (LANES - 1)
        value = jnp.take_along_axis(halves[0], low, axis=1, mode="promise_in_bounds")
        for h in range(1, len(halves)):
            other = jnp.take_along_axis(halves[h], low, axis=1, mode="promise_in_bounds")
            value = jnp.where(idx >= h * LANES, other, value)
        out.append(value)
    return out


def cross(a, b):
    return [
        a[1] * b[2] - a[2] * b[1],
        a[2] * b[0] - a[0] * b[2],
        a[0] * b[1] - a[1] * b[0],
    ]


def edges(verts, corner_ids):
    corners = [[pick_lanes(verts[d], corner_ids[k]) for d in range(3)] for k in range(3)]
    pieces = []
    for h in range(len(corner_ids[0])):
        a, b, c = [[corners[k][d][h] for d in range(3)] for k in range(3)]
        center = [(a[d] + b[d] + c[d]) * (1.0 / 3.0) for d in range(3)]
        one = [b[d] - a[d] for d in range(3)]
        two = [c[d] - a[d] for d in range(3)]
        normal = [0.5 * v for v in cross(one, two)]
        pieces.append((center, one, two, normal))
    return pieces


def root_norm(normal):
    return jnp.sqrt(normal[0] * normal[0] + normal[1] * normal[1] + normal[2] * normal[2] + AREA_SQ)


def kernel(
    cfg,
    x_ref, tris_ref, local_ref, partner_ref, ctrl_ref, mom_hbm, tv_hbm, tt_hbm,
    tg_out, mg_hbm,
    mom, tv, tt, xs, xb, csc, khi, klo, vel, own, tgt, mates, acc, geo, hot, cots, chi, mg, tgs,
    mom_sem, t_sem, xs_s, xs_r, pn_s, pn_r, ct_s, ct_r, tg_s, tg_r, out_sem,
):
    n, nsub, subjects, elems, ctrl, cdev, bits, chunk = cfg
    rows = 3 * subjects
    halves = elems // LANES
    groups = subjects // 8
    me = lax.axis_index("blk")
    sub = lax.axis_index("subj")

    loads = [pltpu.make_async_copy(mom_hbm, mom, mom_sem.at[0])]
    tloads = [
        pltpu.make_async_copy(tv_hbm, tv, t_sem.at[0]),
        pltpu.make_async_copy(tt_hbm, tt, t_sem.at[1]),
    ]
    for c in loads + tloads:
        c.start()

    barrier = pltpu.get_barrier_semaphore()
    for o in range(1, n):
        pl.semaphore_signal(barrier, inc=1, device_id={"blk": me ^ o}, device_id_type=MESH)
    for o in range(1, nsub):
        pl.semaphore_signal(
            barrier, inc=1, device_id={"subj": lax.rem(sub + o, nsub)}, device_id_type=MESH
        )

    def spread(points, slot):
        padded = jnp.concatenate([points * SCALE, jnp.zeros((5, elems), f32)], axis=0)
        columns = padded.T
        for d in range(3):
            xb[slot, d] = jnp.broadcast_to(columns[:, d : d + 1], (elems, LANES))

    spread(x_ref[...], 0)
    csc[...] = ctrl_ref[...] * SCALE
    vel[...] = jnp.zeros_like(vel)

    def kernel_chunk(slot, start):
        cs = [csc[d : d + 1, pl.ds(start, chunk)] for d in range(3)]
        step = 32
        for r in range(0, elems, step):
            total = None
            for d in range(3):
                xv = xb[slot, d, pl.ds(r, step), :]
                off = jnp.concatenate([xv] * (chunk // LANES), axis=1) - cs[d]
                total = off * off if total is None else total + off * off
            hi, lo = split(jnp.exp2(-total))
            khi[pl.ds(r, step), :] = hi
            klo[pl.ds(r, step), :] = lo

    for c in loads:
        c.wait()

    def forward(i, carry):
        start = pl.multiple_of(i * chunk, chunk)
        kernel_chunk(0, start)
        m = mom[:, pl.ds(start, chunk)]
        weighted = [m]
        for d in range(3):
            weighted.append(m * ctrl_ref[d : d + 1, pl.ds(start, chunk)])
        pairs = [split(w) for w in weighted]
        hi = jnp.concatenate([p[0] for p in pairs], axis=0)
        lo = jnp.concatenate([p[1] for p in pairs], axis=0)
        vel[...] += mxu(hi, khi[...], NT) + mxu(lo, khi[...], NT) + mxu(hi, klo[...], NT)
        return carry

    lax.fori_loop(0, ctrl // chunk, forward, 0)

    pl.semaphore_wait(barrier, n - 1 + nsub - 1)

    def to_blk(src, dst, ssem, rsem, o, s):
        return pltpu.make_async_remote_copy(
            src_ref=src, dst_ref=dst, send_sem=ssem.at[s], recv_sem=rsem.at[s],
            device_id={"blk": me ^ o}, device_id_type=MESH,
        )

    x_sends = [to_blk(x_ref, xs.at[o - 1], xs_s, xs_r, o, o - 1) for o in range(1, n)]
    for c in x_sends:
        c.start()

    lane = lambda h: slice(h * LANES, (h + 1) * LANES)
    for g in range(groups):
        verts = [
            [
                x_ref[d : d + 1, lane(h)] + vel[pl.ds(d * subjects + g * 8, 8), lane(h)]
                for h in range(halves)
            ]
            for d in range(3)
        ]
        ids = [
            [jnp.broadcast_to(tris_ref[k : k + 1, lane(h)], (8, LANES)) for h in range(halves)]
            for k in range(3)
        ]
        for h, (center, one, two, normal) in enumerate(edges(verts, ids)):
            nu = root_norm(normal)
            inv = 1.0 / jnp.sqrt(nu)
            for d in range(3):
                own[d, g, h] = center[d] * SCALE
                own[3 + d, g, h] = normal[d] * inv
                geo[d, g, h] = one[d]
                geo[3 + d, g, h] = two[d]
                geo[6 + d, g, h] = normal[d]
            geo[9, g, h] = nu

    p_sends = [to_blk(own, mates.at[b], pn_s, pn_r, 2**b, b) for b in range(bits)]
    for c in p_sends:
        c.start()

    for c in tloads:
        c.wait()
    for g in range(groups):
        part = lambda d: pl.ds(d * subjects + g * 8, 8)
        verts = [[tv[part(d), lane(h)] for h in range(halves)] for d in range(3)]
        ids = [[tt[part(k), lane(h)] for h in range(halves)] for k in range(3)]
        for h, (center, one, two, normal) in enumerate(edges(verts, ids)):
            inv = 1.0 / jnp.sqrt(root_norm(normal))
            for d in range(3):
                tgt[d, g, h] = center[d] * SCALE
                tgt[3 + d, g, h] = normal[d] * inv

    for k in range(3):
        vertex = lax.broadcasted_iota(jnp.int32, (elems, elems), 0)
        hot[:, k * elems : (k + 1) * elems] = jnp.where(
            vertex == tris_ref[k : k + 1, :], 1.0, 0.0
        ).astype(bf16)

    acc[...] = jnp.zeros_like(acc)

    def interact(load, g, a_blocks, coefs):
        q = load()
        p = [[own[d, g, a] for d in range(3)] for a in a_blocks]
        u = [[geo[6 + d, g, a] for d in range(3)] for a in a_blocks]
        unroll = 4

        def body(i, sums):
            sums = list(sums)
            for v in range(unroll):
                shift = i * unroll + v
                rolled = [pltpu.roll(value, shift, 1) for value in q]
                for x in range(len(a_blocks)):
                    off = [p[x][d] - rolled[d] for d in range(3)]
                    weight = jnp.exp2(-(off[0] * off[0] + off[1] * off[1] + off[2] * off[2]))
                    inner = (
                        u[x][0] * rolled[3] + u[x][1] * rolled[4] + u[x][2] * rolled[5]
                    )
                    t = weight * inner
                    s = t * inner
                    for d in range(3):
                        sums[6 * x + d] = sums[6 * x + d] + s * off[d]
                        sums[6 * x + 3 + d] = sums[6 * x + 3 + d] + t * rolled[3 + d]
            return tuple(sums)

        zero = jnp.zeros((8, LANES), f32)
        sums = lax.fori_loop(0, LANES // unroll, body, (zero,) * (6 * len(a_blocks)))
        for x, a in enumerate(a_blocks):
            for d in range(6):
                acc[d, g, a] += coefs[x] * sums[6 * x + d]

    every = list(range(halves))
    as_float = lambda v: v.astype(f32)
    for b in range(halves):
        local = [as_float(local_ref[a, b] + local_ref[b, a]) for a in every]

        def near(g, carry, b=b, local=local):
            interact(lambda: [tgt[d, g, b] for d in range(6)], g, [b], [-2.0])
            interact(lambda: [own[d, g, b] for d in range(6)], g, every, local)
            return carry

        lax.fori_loop(0, groups, near, 0)

    for bit in range(bits):
        p_sends[bit].wait_recv()
        for b in range(halves):
            coefs = []
            for a in every:
                count = jnp.int32(0)
                for r in range(4):
                    if r % (n.bit_length() - 1) == bit:
                        count = count + jnp.where(partner_ref[r, a] == b, 2, 0)
                coefs.append(as_float(count))

            def far(g, carry, b=b, bit=bit, coefs=coefs):
                interact(lambda: [mates[bit, d, g, b] for d in range(6)], g, every, coefs)
                return carry

            lax.fori_loop(0, groups, far, 0)

    width = 1.0 / LANES
    corner = [[[[None] * halves for _ in range(groups)] for _ in range(3)] for _ in range(3)]
    for g in range(groups):
        for h in range(halves):
            one = [geo[d, g, h] for d in range(3)]
            two = [geo[3 + d, g, h] for d in range(3)]
            u = [geo[6 + d, g, h] for d in range(3)]
            inv = 1.0 / geo[9, g, h]
            moved = [acc[d, g, h] for d in range(3)]
            turned = [acc[3 + d, g, h] for d in range(3)]
            total = u[0] * turned[0] + u[1] * turned[1] + u[2] * turned[2]
            shrink = inv * inv * inv * total
            gp = [moved[d] * inv * (-2.0 * width / SCALE / 3.0) for d in range(3)]
            gu = [(2.0 * inv * turned[d] - u[d] * shrink) * (0.5 * width) for d in range(3)]
            g_one = cross(two, gu)
            g_two = cross(gu, one)
            for d in range(3):
                corner[0][d][g][h] = gp[d] - g_one[d] - g_two[d]
                corner[1][d][g][h] = gp[d] + g_one[d]
                corner[2][d][g][h] = gp[d] + g_two[d]
    for k in range(3):
        for h in range(halves):
            column = pl.ds(k * elems + h * LANES, LANES)
            value = jnp.concatenate(
                [corner[k][d][g][h] for d in range(3) for g in range(groups)], axis=0
            )
            hi, lo = split(value)
            chi[0:rows, column] = hi
            chi[rows : 2 * rows, column] = lo
    both = mxu(chi[...], hot[...], NT)
    cot = both[0:rows] + both[rows : 2 * rows]
    cots[0] = cot

    c_sends = [to_blk(cots.at[0], cots.at[o], ct_s, ct_r, o, o - 1) for o in range(1, n)]
    for c in c_sends:
        c.start()

    def over_rows(value):
        return jnp.sum(value, axis=0, keepdims=True)

    plain = over_rows(cot * vel[0:rows, :])
    factor = 1.0 / (subjects * nsub)
    for d in range(3):
        direct = over_rows(cot[d * subjects : (d + 1) * subjects])
        moved = over_rows(cot * vel[(d + 1) * rows : (d + 2) * rows, :])
        tgs[sub, pl.ds(d, 1), :] = factor * (direct - 2.0 * (x_ref[d : d + 1, :] * plain - moved))

    g_sends = []
    for o in range(1, nsub):
        g_sends.append(
            pltpu.make_async_remote_copy(
                src_ref=tgs.at[sub], dst_ref=tgs.at[sub], send_sem=tg_s.at[o - 1],
                recv_sem=tg_r.at[o - 1], device_id={"subj": lax.rem(sub + o, nsub)},
                device_id_type=MESH,
            )
        )
    for c in g_sends:
        c.start()

    for o in range(1, n):
        x_sends[o - 1].wait_recv()
        spread(xs[o - 1], o)

    for o in range(n):
        if o:
            c_sends[o - 1].wait_recv()
        hi, lo = split(cots[o])

        def backward(i, carry, o=o, hi=hi, lo=lo):
            start = pl.multiple_of(i * chunk, chunk)
            kernel_chunk(o, pl.multiple_of(me * cdev + i * chunk, chunk))
            term = mxu(hi, khi[...], NN) + mxu(lo, khi[...], NN) + mxu(hi, klo[...], NN)
            if o:
                mg[:, pl.ds(start, chunk)] += term
            else:
                mg[:, pl.ds(start, chunk)] = term
            return carry

        lax.fori_loop(0, cdev // chunk, backward, 0)

    outs = [pltpu.make_async_copy(mg, mg_hbm, out_sem.at[0])]
    for c in outs:
        c.start()
    for c in g_sends:
        c.wait_recv()
    tg_sum = tgs[0]
    for o in range(1, nsub):
        tg_sum = tg_sum + tgs[o]
    tg_out[...] = tg_sum
    for c in x_sends + p_sends + c_sends + g_sends:
        c.wait_send()
    for c in outs:
        c.wait()


def on_device(n, nsub, tverts, ttris, local, partner, controls, momenta, tv, tt):
    subjects, _, ctrl = momenta.shape
    elems = tverts.shape[1]
    halves = elems // LANES
    groups = subjects // 8
    rows = 3 * subjects
    cdev = ctrl // n
    bits = min(4, n.bit_length() - 1)
    chunk = min(512, cdev)
    cfg = (n, nsub, subjects, elems, ctrl, cdev, bits, chunk)
    vmem = pl.BlockSpec(memory_space=pltpu.VMEM)
    smem = pl.BlockSpec(memory_space=pltpu.SMEM)
    hbm = pl.BlockSpec(memory_space=pl.ANY)
    panel = (6, groups, halves, 8, LANES)
    dma = pltpu.SemaphoreType.DMA
    by_axis = lambda v: v.transpose(1, 0, 2).reshape(rows, v.shape[2])
    template_grad, grads = pl.pallas_call(
        functools.partial(kernel, cfg),
        out_shape=(
            jax.ShapeDtypeStruct((3, elems), f32),
            jax.ShapeDtypeStruct((rows, cdev), f32),
        ),
        in_specs=[vmem, vmem, smem, smem, vmem, hbm, hbm, hbm],
        out_specs=(vmem, hbm),
        scratch_shapes=[
            pltpu.VMEM((rows, ctrl), f32),
            pltpu.VMEM((rows, elems), f32),
            pltpu.VMEM((rows, elems), jnp.int32),
            pltpu.VMEM((n - 1, 3, elems), f32),
            pltpu.VMEM((n, 3, elems, LANES), f32),
            pltpu.VMEM((3, ctrl), f32),
            pltpu.VMEM((elems, chunk), bf16),
            pltpu.VMEM((elems, chunk), bf16),
            pltpu.VMEM((4 * rows, elems), f32),
            pltpu.VMEM(panel, f32),
            pltpu.VMEM(panel, f32),
            pltpu.VMEM((bits,) + panel, f32),
            pltpu.VMEM(panel, f32),
            pltpu.VMEM((10,) + panel[1:], f32),
            pltpu.VMEM((elems, 3 * elems), bf16),
            pltpu.VMEM((n, rows, elems), f32),
            pltpu.VMEM((2 * rows, 3 * elems), bf16),
            pltpu.VMEM((rows, cdev), f32),
            pltpu.VMEM((nsub, 3, elems), f32),
            dma((1,)), dma((2,)),
            dma((n - 1,)), dma((n - 1,)),
            dma((bits,)), dma((bits,)),
            dma((n - 1,)), dma((n - 1,)),
            dma((nsub - 1,)), dma((nsub - 1,)),
            dma((1,)),
        ],
        compiler_params=pltpu.CompilerParams(
            collective_id=0, has_side_effects=True, vmem_limit_bytes=48 * 2**20
        ),
        name="atlas",
    )(tverts, ttris, local, partner, controls, by_axis(momenta), by_axis(tv), by_axis(tt))
    return template_grad, grads.reshape(3, subjects, cdev).transpose(1, 0, 2)


def solution(mesh):
    return jax.shard_map(
        functools.partial(on_device, mesh.shape["blk"], mesh.shape["subj"]),
        mesh=mesh,
        in_specs=(
            P(None, ("groups", "blk")),
            P(None, ("groups", "blk")),
            P("blk", None),
            P(None, "blk"),
            P(),
            P(("groups", "subj"), None, None),
            P(("groups", "subj"), None, "blk"),
            P(("groups", "subj"), None, "blk"),
        ),
        out_specs=(P(None, ("groups", "blk")), P(("groups", "subj"), None, "blk")),
        check_vma=False,
    )
```

profile of v0, /device:TPU:0, one launch (start us, length us, event | category | flops | bytes accessed | tf_op | source)
XLA Modules:
  0.0 85.2 jit_solution(2077238868591573502)
XLA Ops:
  0.6 0.8 copy.10.partner_ref
  1.4 0.0 copy-start
  1.4 1.4 %copy-done = f32[16,3,8192]{2,0,1:T(8,128)S(1)} copy-done((f32[16,3,8192]{2,0,1:T(8,128)S(1)}, f32[16,3,8192]{2,0,1:T(8,128)}, u32[]{:S(2)}) %copy-start) | copy-done | bytes 1572888
  2.8 0.0 copy-start.1
  2.8 0.9 %copy-done.1 = f32[3,8192]{1,0:T(4,128)S(1)} copy-done((f32[3,8192]{1,0:T(4,128)S(1)}, f32[3,8192]{1,0:T(4,128)}, u32[]{:S(2)}) %copy-start.1) | copy-done | bytes 98328
  3.7 0.0 copy-start.2
  3.7 0.8 copy-done.2
  4.5 0.0 copy-start.3
  4.5 0.8 copy-done.3
  5.3 0.0 copy-start.4
  5.3 0.7 copy-done.4
  6.0 0.0 copy-start.5
  6.0 0.7 copy-done.5
  6.7 0.0 copy-start.6
  6.7 0.7 copy-done.6
  7.4 76.5 %atlas.1 = (f32[3,256]{1,0:T(4,128)S(1)}, f32[48,2048]{1,0:T(8,128)S(1)}) custom-call(f32[3,256]{1,0:T(4,128)S(1)} %copy-done.4, s32[3,256]{1,0:T(4,128)S(1)} %copy-done.5, s32[2,2]{1,0:T(2,128)S(1)} %copy-done.6, s32[4,2]{1,0:T(4,128)S(1)} %copy.10.partner_ref, f32[3,8192]{1,0:T(4,128)S(1)} %copy-done.1, f32[48,8192]{1,0:T(8,128)S(1)} %bitcast.12, ...), custom_call_target="tpu_custom_call" | custom-call | tf_op jit(solution)/shard_map/atlas/pallas_call | solution.py:367
  83.8 0.6 copy.13
  84.4 0.7 copy.14
Async XLA Ops:
  1.4 1.4 %copy-start = (f32[16,3,8192]{2,0,1:T(8,128)S(1)}, f32[16,3,8192]{2,0,1:T(8,128)}, u32[]{:S(2)}) copy-start(f32[16,3,8192]{2,0,1:T(8,128)} %param.13) | copy-start | bytes 4718596
  2.8 0.9 %copy-start.1 = (f32[3,8192]{1,0:T(4,128)S(1)}, f32[3,8192]{1,0:T(4,128)}, u32[]{:S(2)}) copy-start(f32[3,8192]{1,0:T(4,128)} %ctrl_ref.1) | copy-start | bytes 294916
  3.7 0.8 copy-start.2
  4.5 0.8 copy-start.3
  5.3 0.7 copy-start.4
  6.0 0.7 copy-start.5
  6.7 0.7 copy-start.6
where the time goes:
time: 85.5 us; the launch traced here: 85.2 us
  Pallas kernels  76.5 us (89%)
  local copies, waits for them, and re-layouts  8.06 us (9%)
    pallas_call x1, Pallas kernels, on_device(): pl.pallas_call(functools.partial(kernel, cfg), out_shape=(jax.ShapeDtypeS...  76.5 us
    unnamed x17, local copies, waits for them, and re-layouts  8.06 us

commit v1 on v0

--- a/solution.py
+++ b/solution.py
@@ -11,6 +11,7 @@
 AREA_SQ = 0.25
 SCALE = math.sqrt(math.log2(math.e))
 LANES = 128
+UNROLL = 64
 MESH = pl.DeviceIdType.MESH
 f32, bf16 = jnp.float32, jnp.bfloat16
 NT = (((1,), (1,)), ((), ()))
@@ -65,9 +66,9 @@
 
 def kernel(
     cfg,
-    x_ref, tris_ref, local_ref, partner_ref, ctrl_ref, mom_hbm, tv_hbm, tt_hbm,
+    x_hbm, tris_hbm, local_hbm, partner_hbm, ctrl_hbm, mom_hbm, tv_hbm, tt_hbm,
     tg_out, mg_hbm,
-    mom, tv, tt, xs, xb, csc, khi, klo, vel, own, tgt, mates, acc, geo, hot, cots, chi, mg, tgs,
+    x_ref, tris_ref, local_ref, partner_ref, ctrl_ref, mom, tv, tt, xs, xb, csc, khi, klo, vel, own, tgt, mates, acc, geo, hot, cots, chi, mg, tgs,
     mom_sem, t_sem, xs_s, xs_r, pn_s, pn_r, ct_s, ct_r, tg_s, tg_r, out_sem,
 ):
     n, nsub, subjects, elems, ctrl, cdev, bits, chunk = cfg
@@ -77,10 +78,17 @@
     me = lax.axis_index("blk")
     sub = lax.axis_index("subj")
 
-    loads = [pltpu.make_async_copy(mom_hbm, mom, mom_sem.at[0])]
+    loads = [
+        pltpu.make_async_copy(x_hbm, x_ref, mom_sem.at[0]),
+        pltpu.make_async_copy(ctrl_hbm, ctrl_ref, mom_sem.at[1]),
+        pltpu.make_async_copy(mom_hbm, mom, mom_sem.at[2]),
+    ]
     tloads = [
-        pltpu.make_async_copy(tv_hbm, tv, t_sem.at[0]),
-        pltpu.make_async_copy(tt_hbm, tt, t_sem.at[1]),
+        pltpu.make_async_copy(tris_hbm, tris_ref, t_sem.at[0]),
+        pltpu.make_async_copy(tv_hbm, tv, t_sem.at[1]),
+        pltpu.make_async_copy(tt_hbm, tt, t_sem.at[2]),
+        pltpu.make_async_copy(local_hbm, local_ref, t_sem.at[3]),
+        pltpu.make_async_copy(partner_hbm, partner_ref, t_sem.at[4]),
     ]
     for c in loads + tloads:
         c.start()
@@ -99,7 +107,9 @@
         for d in range(3):
             xb[slot, d] = jnp.broadcast_to(columns[:, d : d + 1], (elems, LANES))
 
+    loads[0].wait()
     spread(x_ref[...], 0)
+    loads[1].wait()
     csc[...] = ctrl_ref[...] * SCALE
     vel[...] = jnp.zeros_like(vel)
 
@@ -116,8 +126,7 @@
             khi[pl.ds(r, step), :] = hi
             klo[pl.ds(r, step), :] = lo
 
-    for c in loads:
-        c.wait()
+    loads[2].wait()
 
     def forward(i, carry):
         start = pl.multiple_of(i * chunk, chunk)
@@ -146,6 +155,7 @@
     for c in x_sends:
         c.start()
 
+    tloads[0].wait()
     lane = lambda h: slice(h * LANES, (h + 1) * LANES)
     for g in range(groups):
         verts = [
@@ -174,7 +184,7 @@
     for c in p_sends:
         c.start()
 
-    for c in tloads:
+    for c in tloads[1:]:
         c.wait()
     for g in range(groups):
         part = lambda d: pl.ds(d * subjects + g * 8, 8)
@@ -194,17 +204,16 @@
 
     acc[...] = jnp.zeros_like(acc)
 
-    def interact(load, g, a_blocks, coefs):
-        q = load()
+    def interact(q, g, a_blocks, coefs):
         p = [[own[d, g, a] for d in range(3)] for a in a_blocks]
         u = [[geo[6 + d, g, a] for d in range(3)] for a in a_blocks]
-        unroll = 4
+        unroll = UNROLL
 
         def body(i, sums):
             sums = list(sums)
             for v in range(unroll):
-                shift = i * unroll + v
-                rolled = [pltpu.roll(value, shift, 1) for value in q]
+                shift = v if unroll == LANES else i * unroll + v
+                rolled = [pltpu.roll(value, shift, 1) if v or unroll < LANES else value for value in q]
                 for x in range(len(a_blocks)):
                     off = [p[x][d] - rolled[d] for d in range(3)]
                     weight = jnp.exp2(-(off[0] * off[0] + off[1] * off[1] + off[2] * off[2]))
@@ -218,40 +227,48 @@
                         sums[6 * x + 3 + d] = sums[6 * x + 3 + d] + t * rolled[3 + d]
             return tuple(sums)
 
-        zero = jnp.zeros((8, LANES), f32)
-        sums = lax.fori_loop(0, LANES // unroll, body, (zero,) * (6 * len(a_blocks)))
+        sums = (jnp.zeros((8, LANES), f32),) * (6 * len(a_blocks))
+        if unroll == LANES:
+            sums = body(0, sums)
+        else:
+            sums = lax.fori_loop(0, LANES // unroll, body, sums)
         for x, a in enumerate(a_blocks):
             for d in range(6):
                 acc[d, g, a] += coefs[x] * sums[6 * x + d]
 
     every = list(range(halves))
     as_float = lambda v: v.astype(f32)
-    for b in range(halves):
+
+    def near_target(i, carry):
+        b, g = i // groups, i % groups
+        interact([tgt[d, g, b] for d in range(6)], g, [b], [-2.0])
+        return carry
+
+    def near_own(i, carry):
+        b, g = i // groups, i % groups
         local = [as_float(local_ref[a, b] + local_ref[b, a]) for a in every]
-
-        def near(g, carry, b=b, local=local):
-            interact(lambda: [tgt[d, g, b] for d in range(6)], g, [b], [-2.0])
-            interact(lambda: [own[d, g, b] for d in range(6)], g, every, local)
-            return carry
-
-        lax.fori_loop(0, groups, near, 0)
+        interact([own[d, g, b] for d in range(6)], g, every, local)
+        return carry
+
+    lax.fori_loop(0, halves * groups, near_target, 0)
+    lax.fori_loop(0, halves * groups, near_own, 0)
 
     for bit in range(bits):
         p_sends[bit].wait_recv()
-        for b in range(halves):
+
+        def far(i, carry, bit=bit):
+            b, g = i // groups, i % groups
             coefs = []
             for a in every:
                 count = jnp.int32(0)
                 for r in range(4):
                     if r % (n.bit_length() - 1) == bit:
-                        count = count + jnp.where(partner_ref[r, a] == b, 2, 0)
+                        count = count + jnp.where(partner_ref[a, r] == b, 2, 0)
                 coefs.append(as_float(count))
-
-            def far(g, carry, b=b, bit=bit, coefs=coefs):
-                interact(lambda: [mates[bit, d, g, b] for d in range(6)], g, every, coefs)
-                return carry
-
-            lax.fori_loop(0, groups, far, 0)
+            interact([mates[bit, d, g, b] for d in range(6)], g, every, coefs)
+            return carry
+
+        lax.fori_loop(0, halves * groups, far, 0)
 
     width = 1.0 / LANES
     corner = [[[[None] * halves for _ in range(groups)] for _ in range(3)] for _ in range(3)]
@@ -359,8 +376,7 @@
     chunk = min(512, cdev)
     cfg = (n, nsub, subjects, elems, ctrl, cdev, bits, chunk)
     vmem = pl.BlockSpec(memory_space=pltpu.VMEM)
-    smem = pl.BlockSpec(memory_space=pltpu.SMEM)
-    hbm = pl.BlockSpec(memory_space=pl.ANY)
+    hbm = pl.BlockSpec(memory_space=pltpu.HBM)
     panel = (6, groups, halves, 8, LANES)
     dma = pltpu.SemaphoreType.DMA
     by_axis = lambda v: v.transpose(1, 0, 2).reshape(rows, v.shape[2])
@@ -370,9 +386,14 @@
             jax.ShapeDtypeStruct((3, elems), f32),
             jax.ShapeDtypeStruct((rows, cdev), f32),
         ),
-        in_specs=[vmem, vmem, smem, smem, vmem, hbm, hbm, hbm],
+        in_specs=[hbm] * 8,
         out_specs=(vmem, hbm),
         scratch_shapes=[
+            pltpu.VMEM((3, elems), f32),
+            pltpu.VMEM((3, elems), jnp.int32),
+            pltpu.SMEM(local.shape, jnp.int32),
+            pltpu.SMEM(partner.shape[::-1], jnp.int32),
+            pltpu.VMEM((3, ctrl), f32),
             pltpu.VMEM((rows, ctrl), f32),
             pltpu.VMEM((rows, elems), f32),
             pltpu.VMEM((rows, elems), jnp.int32),
@@ -392,7 +413,7 @@
             pltpu.VMEM((2 * rows, 3 * elems), bf16),
             pltpu.VMEM((rows, cdev), f32),
             pltpu.VMEM((nsub, 3, elems), f32),
-            dma((1,)), dma((2,)),
+            dma((3,)), dma((5,)),
             dma((n - 1,)), dma((n - 1,)),
             dma((bits,)), dma((bits,)),
             dma((n - 1,)), dma((n - 1,)),
@@ -400,10 +421,10 @@
             dma((1,)),
         ],
         compiler_params=pltpu.CompilerParams(
-            collective_id=0, has_side_effects=True, vmem_limit_bytes=48 * 2**20
+            collective_id=0, has_side_effects=True, vmem_limit_bytes=64 * 2**20
         ),
         name="atlas",
-    )(tverts, ttris, local, partner, controls, by_axis(momenta), by_axis(tv), by_axis(tt))
+    )(tverts, ttris, local, partner.T, controls, by_axis(momenta), by_axis(tv), by_axis(tt))
     return template_grad, grads.reshape(3, subjects, cdev).transpose(1, 0, 2)
 
 

time: 85.5 us -> 45.8 us (0.54)
  Pallas kernels: 76.5 us -> 41.9 us
  local copies, waits for them, and re-layouts: 8.06 us -> 3.03 us
    pallas_call x1, Pallas kernels: 76.5 us -> 41.9 us  [on_device(): pl.pallas_call(functools.partial(kernel, cfg), out_shape=(jax.ShapeDtypeS...]
    unnamed x17 -> x2, local copies, waits for them, and re-layouts: 8.06 us -> 3.03 us
where the time goes in v1:
time: 45.8 us; the launch traced here: 45.5 us
  Pallas kernels  41.9 us (91%)
  local copies, waits for them, and re-layouts  3.03 us (7%)
  between operations  0.64 us (1%)
    pallas_call x1, Pallas kernels, on_device(): pl.pallas_call(functools.partial(kernel, cfg), out_shape=(jax.ShapeDtypeS...  41.9 us
    unnamed x2, local copies, waits for them, and re-layouts  3.03 us

profile of v1, /device:TPU:0, one launch (start us, length us, event | category | flops | bytes accessed | tf_op | source)
XLA Modules:
  0.0 45.5 jit_solution(4086463798473410106)
XLA Ops:
  0.6 41.9 %atlas.1 = (f32[3,256]{1,0:T(4,128)}, f32[48,2048]{1,0:T(8,128)}) custom-call(f32[3,256]{1,0:T(4,128)} %x_hbm.1, s32[3,256]{1,0:T(4,128)} %tris_hbm.1, s32[2,2]{1,0:T(2,128)} %local_hbm.1, s32[2,4]{1,0:T(2,128)} %bitcast.17, f32[3,8192]{1,0:T(4,128)} %ctrl_hbm.1, f32[48,8192]{1,0:T(8,128)} %bitcast.13, f32[48,256]{1,0:T(8,128)} %bitcast.15, s32[48,256]{1,0:T(8,128)} %bitcast.16), custom_call_target="tpu_custom_call" | custom-call | tf_op jit(solution)/shard_map/atlas/pallas_call | solution.py:383
  42.5 1.3 %copy.12 = f32[3,256]{1,0:T(4,128)} copy(f32[3,256]{1,0:T(4,128)} %get-tuple-element.8) | data formatting | bytes 6144
  43.8 1.8 %copy.13 = f32[16,3,2048]{2,0,1:T(8,128)} copy(f32[16,3,2048]{2,0,1:T(8,128)} %bitcast.14) | data formatting | bytes 786432

commit v2 on v1

--- a/solution.py
+++ b/solution.py
@@ -68,7 +68,7 @@
     cfg,
     x_hbm, tris_hbm, local_hbm, partner_hbm, ctrl_hbm, mom_hbm, tv_hbm, tt_hbm,
     tg_out, mg_hbm,
-    x_ref, tris_ref, local_ref, partner_ref, ctrl_ref, mom, tv, tt, xs, xb, csc, khi, klo, vel, own, tgt, mates, acc, geo, hot, cots, chi, mg, tgs,
+    x_ref, tris_ref, local_ref, partner_ref, ctrl_ref, mom, tv, tt, xs, xb, csc, khi, klo, khi_b, klo_b, bhi, blo, vel, own, tgt, mates, acc, geo, hot, cots, chi, mg, tgs,
     mom_sem, t_sem, xs_s, xs_r, pn_s, pn_r, ct_s, ct_r, tg_s, tg_r, out_sem,
 ):
     n, nsub, subjects, elems, ctrl, cdev, bits, chunk = cfg
@@ -113,7 +113,7 @@
     csc[...] = ctrl_ref[...] * SCALE
     vel[...] = jnp.zeros_like(vel)
 
-    def kernel_chunk(slot, start):
+    def kernel_chunk(slot, start, hi_to, lo_to):
         cs = [csc[d : d + 1, pl.ds(start, chunk)] for d in range(3)]
         step = 32
         for r in range(0, elems, step):
@@ -123,25 +123,33 @@
                 off = jnp.concatenate([xv] * (chunk // LANES), axis=1) - cs[d]
                 total = off * off if total is None else total + off * off
             hi, lo = split(jnp.exp2(-total))
-            khi[pl.ds(r, step), :] = hi
-            klo[pl.ds(r, step), :] = lo
+            hi_to[pl.ds(r, step), :] = hi
+            lo_to[pl.ds(r, step), :] = lo
 
     loads[2].wait()
 
-    def forward(i, carry):
-        start = pl.multiple_of(i * chunk, chunk)
-        kernel_chunk(0, start)
+    def weigh(start, hi_from, lo_from):
         m = mom[:, pl.ds(start, chunk)]
         weighted = [m]
         for d in range(3):
             weighted.append(m * ctrl_ref[d : d + 1, pl.ds(start, chunk)])
         pairs = [split(w) for w in weighted]
         hi = jnp.concatenate([p[0] for p in pairs], axis=0)
-        lo = jnp.concatenate([p[1] for p in pairs], axis=0)
-        vel[...] += mxu(hi, khi[...], NT) + mxu(lo, khi[...], NT) + mxu(hi, klo[...], NT)
+        both = mxu(jnp.concatenate([hi] + [p[1] for p in pairs], axis=0), hi_from[...], NT)
+        vel[...] += both[0 : 4 * rows] + both[4 * rows :] + mxu(hi, lo_from[...], NT)
+
+    at = lambda i: pl.multiple_of(i * chunk, chunk)
+    steps = ctrl // chunk
+    kernel_chunk(0, 0, khi, klo)
+
+    def forward(i, carry):
+        kernel_chunk(0, at(2 * i + 1), khi_b, klo_b)
+        weigh(at(2 * i), khi, klo)
+        kernel_chunk(0, at(jnp.minimum(2 * i + 2, steps - 1)), khi, klo)
+        weigh(at(2 * i + 1), khi_b, klo_b)
         return carry
 
-    lax.fori_loop(0, ctrl // chunk, forward, 0)
+    lax.fori_loop(0, steps // 2, forward, 0)
 
     pl.semaphore_wait(barrier, n - 1 + nsub - 1)
 
@@ -333,22 +341,31 @@
         x_sends[o - 1].wait_recv()
         spread(xs[o - 1], o)
 
-    for o in range(n):
-        if o:
-            c_sends[o - 1].wait_recv()
-        hi, lo = split(cots[o])
-
-        def backward(i, carry, o=o, hi=hi, lo=lo):
-            start = pl.multiple_of(i * chunk, chunk)
-            kernel_chunk(o, pl.multiple_of(me * cdev + i * chunk, chunk))
-            term = mxu(hi, khi[...], NN) + mxu(lo, khi[...], NN) + mxu(hi, klo[...], NN)
-            if o:
-                mg[:, pl.ds(start, chunk)] += term
-            else:
-                mg[:, pl.ds(start, chunk)] = term
+    def backward(make, use):
+        if use is not None:
+            hi, lo = split(cots[use])
+            two = jnp.concatenate([hi, lo], axis=0)
+
+        def body(i, carry):
+            here = pl.ds(at(i), chunk)
+            if make is not None:
+                start = pl.multiple_of(me * cdev + i * chunk, chunk)
+                kernel_chunk(make, start, bhi.at[make, :, here], blo.at[make, :, here])
+            if use is not None:
+                both = mxu(two, bhi[use, :, here], NN)
+                term = both[0:rows] + both[rows:] + mxu(hi, blo[use, :, here], NN)
+                mg[:, here] = mg[:, here] + term if use else term
             return carry
 
-        lax.fori_loop(0, cdev // chunk, backward, 0)
+        lax.fori_loop(0, cdev // chunk, body, 0)
+
+    backward(0, None)
+    backward(1, 0)
+    if n > 2:
+        backward(2, None)
+    for o in range(1, n):
+        c_sends[o - 1].wait_recv()
+        backward(o + 2 if o + 2 < n else None, o)
 
     outs = [pltpu.make_async_copy(mg, mg_hbm, out_sem.at[0])]
     for c in outs:
@@ -402,6 +419,10 @@
             pltpu.VMEM((3, ctrl), f32),
             pltpu.VMEM((elems, chunk), bf16),
             pltpu.VMEM((elems, chunk), bf16),
+            pltpu.VMEM((elems, chunk), bf16),
+            pltpu.VMEM((elems, chunk), bf16),
+            pltpu.VMEM((n, elems, cdev), bf16),
+            pltpu.VMEM((n, elems, cdev), bf16),
             pltpu.VMEM((4 * rows, elems), f32),
             pltpu.VMEM(panel, f32),
             pltpu.VMEM(panel, f32),

time: 45.8 us -> 42.6 us (0.930)
  Pallas kernels: 41.9 us -> 38.7 us
    pallas_call x1, Pallas kernels: 41.9 us -> 38.7 us  [on_device(): pl.pallas_call(functools.partial(kernel, cfg), out_shape=(jax.ShapeDtypeS...]
where the time goes in v2:
time: 42.6 us; the launch traced here: 42.4 us
  Pallas kernels  38.7 us (91%)
  local copies, waits for them, and re-layouts  3.03 us (7%)
  between operations  0.64 us (2%)
    pallas_call x1, Pallas kernels, on_device(): pl.pallas_call(functools.partial(kernel, cfg), out_shape=(jax.ShapeDtypeS...  38.7 us
    unnamed x2, local copies, waits for them, and re-layouts  3.03 us

profile of v2, /device:TPU:0, one launch (start us, length us, event | category | flops | bytes accessed | tf_op | source)
XLA Modules:
  0.0 42.4 jit_solution(7651720927816411548)
XLA Ops:
  0.6 38.7 %atlas.1 = (f32[3,256]{1,0:T(4,128)}, f32[48,2048]{1,0:T(8,128)}) custom-call(f32[3,256]{1,0:T(4,128)} %x_hbm.1, s32[3,256]{1,0:T(4,128)} %tris_hbm.1, s32[2,2]{1,0:T(2,128)} %local_hbm.1, s32[2,4]{1,0:T(2,128)} %bitcast.17, f32[3,8192]{1,0:T(4,128)} %ctrl_hbm.1, f32[48,8192]{1,0:T(8,128)} %bitcast.13, f32[48,256]{1,0:T(8,128)} %bitcast.15, s32[48,256]{1,0:T(8,128)} %bitcast.16), custom_call_target="tpu_custom_call" | custom-call | tf_op jit(solution)/shard_map/atlas/pallas_call | solution.py:400
  39.4 1.3 %copy.12 = f32[3,256]{1,0:T(4,128)} copy(f32[3,256]{1,0:T(4,128)} %get-tuple-element.8) | data formatting | bytes 6144
  40.6 1.8 %copy.13 = f32[16,3,2048]{2,0,1:T(8,128)} copy(f32[16,3,2048]{2,0,1:T(8,128)} %bitcast.14) | data formatting | bytes 786432

commit v3 on v2

--- a/solution.py
+++ b/solution.py
@@ -11,7 +11,7 @@
 AREA_SQ = 0.25
 SCALE = math.sqrt(math.log2(math.e))
 LANES = 128
-UNROLL = 64
+UNROLL = 128
 MESH = pl.DeviceIdType.MESH
 f32, bf16 = jnp.float32, jnp.bfloat16
 NT = (((1,), (1,)), ((), ()))

time: 42.6 us -> 41.8 us (0.981)
  Pallas kernels: 38.7 us -> 37.9 us
    pallas_call x1, Pallas kernels: 38.7 us -> 37.9 us  [on_device(): pl.pallas_call(functools.partial(kernel, cfg), out_shape=(jax.ShapeDtypeS...]
where the time goes in v3:
time: 41.8 us; the launch traced here: 41.6 us
  Pallas kernels  37.9 us (91%)
  local copies, waits for them, and re-layouts  3.03 us (7%)
  between operations  0.64 us (2%)
    pallas_call x1, Pallas kernels, on_device(): pl.pallas_call(functools.partial(kernel, cfg), out_shape=(jax.ShapeDtypeS...  37.9 us
    unnamed x2, local copies, waits for them, and re-layouts  3.03 us

profile of v3, /device:TPU:0, one launch (start us, length us, event | category | flops | bytes accessed | tf_op | source)
XLA Modules:
  0.0 41.6 jit_solution(9632588922411694048)
XLA Ops:
  0.6 37.9 %atlas.1 = (f32[3,256]{1,0:T(4,128)}, f32[48,2048]{1,0:T(8,128)}) custom-call(f32[3,256]{1,0:T(4,128)} %x_hbm.1, s32[3,256]{1,0:T(4,128)} %tris_hbm.1, s32[2,2]{1,0:T(2,128)} %local_hbm.1, s32[2,4]{1,0:T(2,128)} %bitcast.17, f32[3,8192]{1,0:T(4,128)} %ctrl_hbm.1, f32[48,8192]{1,0:T(8,128)} %bitcast.13, f32[48,256]{1,0:T(8,128)} %bitcast.15, s32[48,256]{1,0:T(8,128)} %bitcast.16), custom_call_target="tpu_custom_call" | custom-call | tf_op jit(solution)/shard_map/atlas/pallas_call | solution.py:400
  38.6 1.3 %copy.12 = f32[3,256]{1,0:T(4,128)} copy(f32[3,256]{1,0:T(4,128)} %get-tuple-element.8) | data formatting | bytes 6144
  39.8 1.8 %copy.13 = f32[16,3,2048]{2,0,1:T(8,128)} copy(f32[16,3,2048]{2,0,1:T(8,128)} %bitcast.14) | data formatting | bytes 786432
